TPU v7x, 256 devices: a whole 4x4x8 slice. The times are simulated.
256 devices in a mesh: expert: 64 (over z, y, core), dp: 4 (over x).
Axes of the slice: x: 4, y: 4, z: 8, core: 2. Of those that a mesh axis runs over, the one named last changes fastest.
Arguments:
- prenorm_input: bfloat16 [32768, 1280], P(('expert', 'dp')), may hold values from -6 to 6
- gain: float32 [1280], replicated, may hold values from 0.25 to 1.75
- router: bfloat16 [1280, 32], replicated, may hold values from -0.15625 to 0.15625
- routes: int32 [32768, 2], P(('expert', 'dp')), may hold values from 0 to 31, all different within a row; in each aligned block of 128 rows (0 to 127, 128 to 255, ...) at most 10 rows name the same one
- w_in: bfloat16 [64, 1280, 1280], P('expert', None, 'dp'), may hold values from -0.15625 to 0.15625
- w_out: bfloat16 [64, 1280, 1280], P('expert', 'dp'), may hold values from -0.125 to 0.125
- cotangent: bfloat16 [32768, 1280], P(('expert', 'dp')), may hold values from -18 to 18
Outputs:
- input_grad: bfloat16 [32768, 1280], P(('expert', 'dp'))
- grad_in: bfloat16 [64, 1280, 1280], P('expert', None, 'dp')
- grad_out: bfloat16 [64, 1280, 1280], P('expert', 'dp')
- grad_router: float32 [1280, 32], replicated
- grad_gain: float32 [1280], replicated
Inputs may be any that keep to these rules, and one draw needn't show every extreme that they name: `routes`: each row names 2 different experts; among the rows of one device no expert is named more than 10 times.
All inputs are finite; a program needn't handle non-finite values.
Results may differ from a plain program's by a relative error of at most 0.015.
Values may be sent and summed in bfloat16 or wider, within the bound.
A program may use at most 128 MiB of HBM per device.

v0:
```python
import math
import jax
import jax.numpy as jnp
from jax import lax
from jax.sharding import PartitionSpec as P


def gelu_parts(pre):
    coeff = math.sqrt(2.0 / math.pi)
    inner = coeff * (pre + 0.044715 * pre * pre * pre)
    tanh_val = jnp.tanh(inner)
    value = 0.5 * pre * (1.0 + tanh_val)
    slope = 0.5 * (1.0 + tanh_val) + 0.5 * pre * (1.0 - tanh_val * tanh_val) * coeff * (
        1.0 + 3.0 * 0.044715 * pre * pre
    )
    return (value, slope)


def norm_pieces(block, gain):
    values = block.astype(jnp.float32)
    centred_rows = values - jnp.mean(values, axis=1, keepdims=True)
    inverse_deviation = lax.rsqrt(
        jnp.mean(centred_rows * centred_rows, axis=1, keepdims=True) + 1e-06
    )
    normalized_rows = centred_rows * inverse_deviation
    return (
        normalized_rows,
        inverse_deviation,
        (normalized_rows * gain[None, :]).astype(jnp.bfloat16),
    )


def slot_index(routing_rows, expert_list, expert_capacity):
    flat = routing_rows.reshape(-1)
    onehot = (flat[:, None] == jnp.arange(expert_list, dtype=jnp.int32)[None, :]).astype(jnp.int32)
    before = jnp.cumsum(onehot, axis=0) - onehot
    slot = jnp.sum(before * onehot, axis=1)
    return flat * expert_capacity + slot


def expert_pass(rows_m, rows_d, column, w_first, w_second):
    gate = jax.nn.sigmoid(jnp.dot(rows_m, column, preferred_element_type=jnp.float32)[:, 0])
    pre = jnp.dot(rows_m, w_first, preferred_element_type=jnp.float32)
    value, slope = gelu_parts(pre)
    hidden = value.astype(jnp.bfloat16)
    back = jnp.dot(rows_d, w_second.T, preferred_element_type=jnp.float32)
    gate_gradient = jnp.sum(hidden.astype(jnp.float32) * back, axis=1)
    grad_pre = (gate[:, None] * back * slope).astype(jnp.bfloat16)
    grad_y = (gate[:, None] * rows_d.astype(jnp.float32)).astype(jnp.bfloat16)
    grad_second = jnp.dot(hidden.T, grad_y, preferred_element_type=jnp.float32)
    grad_first = jnp.dot(rows_m.T, grad_pre, preferred_element_type=jnp.float32)
    row_gradient = jnp.dot(grad_pre, w_first.T, preferred_element_type=jnp.float32)
    return (row_gradient, gate_gradient, grad_first, grad_second)


def body(prenorm_input, gain, router, routes, w_in, w_out, cotangent):
    halves = lax.axis_size("expert")
    expert_list = halves // 2
    groups = lax.axis_size("dp")
    tok_rows = prenorm_input.shape[0]
    top = routes.shape[1]
    width = prenorm_input.shape[1]
    expert_capacity = max(2, 5 * tok_rows * top // (4 * expert_list))
    slots = expert_list * expert_capacity
    hi = lax.Precision.HIGHEST
    normalized_rows, inverse_deviation, mixed_rows = norm_pieces(prenorm_input, gain)
    where = slot_index(routes, expert_list, expert_capacity)
    places = (where[None, :] == jnp.arange(slots, dtype=jnp.int32)[:, None]).astype(jnp.bfloat16)
    send_m = jnp.dot(
        places, jnp.repeat(mixed_rows, top, axis=0), preferred_element_type=jnp.float32
    ).astype(jnp.bfloat16)
    send_d = jnp.dot(
        places, jnp.repeat(cotangent, top, axis=0), preferred_element_type=jnp.float32
    ).astype(jnp.bfloat16)
    send_m = jnp.repeat(send_m.reshape(expert_list, expert_capacity, width), 2, axis=0)
    send_d = jnp.repeat(send_d.reshape(expert_list, expert_capacity, width), 2, axis=0)
    recv_m, recv_d = (
        lax.all_to_all(send_m, "expert", split_axis=0, concat_axis=0, tiled=True),
        lax.all_to_all(send_d, "expert", split_axis=0, concat_axis=0, tiled=True),
    )
    own = lax.axis_index("expert") // 2
    column = lax.dynamic_slice_in_dim(router, own, 1, 1)
    all_m, all_d = (
        lax.all_gather(recv_m[None], "dp", axis=0, tiled=True),
        lax.all_gather(recv_d[None], "dp", axis=0, tiled=True),
    )
    row_gradient, gate_gradient, grad_first, grad_second = expert_pass(
        all_m.reshape(-1, width), all_d.reshape(-1, width), column, w_in[0], w_out[0]
    )
    summed_rows, summed_gate = (
        lax.psum_scatter(
            row_gradient.reshape(groups, halves * expert_capacity, width).astype(jnp.bfloat16),
            "dp",
            scatter_dimension=0,
            tiled=True,
        ).astype(jnp.float32),
        lax.psum_scatter(
            gate_gradient.reshape(groups, halves * expert_capacity).astype(jnp.bfloat16),
            "dp",
            scatter_dimension=0,
            tiled=True,
        ).astype(jnp.float32),
    )
    back_rows = summed_rows[0].reshape(halves, expert_capacity, width)
    back_gate = summed_gate[0].reshape(halves, expert_capacity)
    grad_in = grad_first[None].astype(jnp.bfloat16)
    grad_out = grad_second[None].astype(jnp.bfloat16)
    ret_rows, ret_gate = (
        lax.all_to_all(
            back_rows.astype(jnp.bfloat16), "expert", split_axis=0, concat_axis=0, tiled=True
        ).astype(back_rows.dtype),
        lax.all_to_all(
            back_gate.astype(jnp.bfloat16), "expert", split_axis=0, concat_axis=0, tiled=True
        ).astype(back_gate.dtype),
    )
    pair_rows = jnp.sum(ret_rows.reshape(expert_list, 2, expert_capacity, width), axis=1).reshape(
        slots, width
    )
    pair_gate = jnp.sum(ret_gate.reshape(expert_list, 2, expert_capacity), axis=1).reshape(slots)
    grad_expert = jnp.sum(jnp.take(pair_rows, where, axis=0).reshape(tok_rows, top, width), axis=1)
    dgate_tok = jnp.take(pair_gate, where, axis=0).reshape(tok_rows, top)
    logits = jnp.dot(mixed_rows, router, preferred_element_type=jnp.float32)
    choose = (routes[:, :, None] == jnp.arange(expert_list, dtype=jnp.int32)[None, None, :]).astype(
        jnp.float32
    )
    gates = jax.nn.sigmoid(jnp.sum(choose * logits[:, None, :], axis=2))
    dlogit = jnp.sum(choose * (dgate_tok * gates * (1.0 - gates))[:, :, None], axis=1)
    mixed_gradient = grad_expert + jnp.dot(dlogit, router.astype(jnp.float32).T, precision=hi)
    router_term = jnp.dot(mixed_rows.astype(jnp.float32).T, dlogit, precision=hi)
    gain_product = jnp.sum(mixed_gradient * normalized_rows, axis=0)
    grad_router, grad_gain = lax.psum((router_term, gain_product), ("expert", "dp"))
    scaled_rows = mixed_gradient * gain[None, :]
    mean_first_term = jnp.mean(scaled_rows, axis=1, keepdims=True)
    mean_second_term = jnp.mean(scaled_rows * normalized_rows, axis=1, keepdims=True)
    norm_backward = inverse_deviation * (
        scaled_rows - mean_first_term - normalized_rows * mean_second_term
    )
    input_grad = (cotangent.astype(jnp.float32) + norm_backward).astype(jnp.bfloat16)
    return (input_grad, grad_in, grad_out, grad_router, grad_gain)


def solution(mesh):
    in_specs = (
        P(("expert", "dp"), None),
        P(),
        P(),
        P(("expert", "dp"), None),
        P("expert", None, "dp"),
        P("expert", "dp", None),
        P(("expert", "dp"), None),
    )
    out_specs = (
        P(("expert", "dp"), None),
        P("expert", None, "dp"),
        P("expert", "dp", None),
        P(),
        P(),
    )
    return jax.shard_map(body, mesh=mesh, in_specs=in_specs, out_specs=out_specs, check_vma=False)
```

profile of v0, /device:TPU:1, one launch (start us, length us, event | category | flops | bytes accessed | tf_op | source)
XLA Modules:
  0.0 642.1 jit_solution(16606466589608056609)
XLA Ops:
  7.2 0.9 copy.48
  8.4 0.6 reduce-window.6
  9.3 1.1 convert_reduce_fusion.1
  10.4 1.2 fusion.32
  11.6 1.2 fusion.25
  12.9 0.7 copy-done.3
  13.6 0.3 broadcast_in_dim.29
  13.9 0.2 reshape.180
  14.2 0.4 convolution_convert_fusion.3
  14.6 0.3 reshape.181
  15.1 75.7 %all_to_all.21 = bf16[64,10,1280]{2,1,0:T(8,128)(2,1)S(1)} all-to-all(bf16[64,10,1280]{2,1,0:T(8,128)(2,1)S(1)} %bitcast.60), channel_id=1, replica_groups=mesh['expert'=64,'dp'=4] {'expert'}, dimensions={0} | all-to-all | bytes 3276800 | tf_op jit(solution)/shard_map/all_to_all | solution.py:78
  90.8 1.7 copy.53
  92.5 0.3 broadcast_in_dim.32
  93.1 0.4 convolution_convert_fusion.2
  93.5 0.3 reshape.186
  94.1 68.1 %all_to_all.22 = bf16[64,10,1280]{2,1,0:T(8,128)(2,1)S(1)} all-to-all(bf16[64,10,1280]{2,1,0:T(8,128)(2,1)S(1)} %bitcast.61), channel_id=1, replica_groups=mesh['expert'=64,'dp'=4] {'expert'}, dimensions={0} | all-to-all | bytes 3276800 | tf_op jit(solution)/shard_map/all_to_all | solution.py:79
  162.2 1.6 copy.55
  163.9 11.2 %copy.54 = bf16[256,10,1280]{2,1,0:T(8,128)(2,1)} copy(bf16[256,10,1280]{2,0,1:T(8,128)(2,1)} %all-gather.5.cloned.1.call-done) | data formatting | bytes 13107200 | tf_op jit(solution)/shard_map/all_gather | solution.py:84
  175.2 13.0 %reshape.183 = bf16[2560,1280]{1,0:T(8,128)(2,1)} reshape(bf16[256,10,1280]{2,1,0:T(8,128)(2,1)} %copy.54) | data formatting | bytes 13107200 | tf_op jit(solution)/shard_map/reshape | solution.py:88
  188.2 4.9 convolution_reduce_fusion
  193.2 4.1 fusion.15
  197.2 34.7 %all-gather.7.cloned.1.call-done = bf16[256,10,1280]{2,0,1:T(8,128)(2,1)} async-done(((bf16[64,10,1280]{2,0,1:T(8,128)(2,1)}), bf16[256,10,1280]{2,0,1:T(8,128)(2,1)}) %all-gather.7.cloned.1.call-update) | async-done | bytes 6553616 | tf_op jit(solution)/shard_map/all_gather | solution.py:85
  231.9 10.8 %copy.56 = bf16[256,10,1280]{2,1,0:T(8,128)(2,1)} copy(bf16[256,10,1280]{2,0,1:T(8,128)(2,1)} %all-gather.7.cloned.1.call-done) | data formatting | bytes 13107200 | tf_op jit(solution)/shard_map/all_gather | solution.py:85
  242.8 12.8 %reshape.188 = bf16[2560,1280]{1,0:T(8,128)(2,1)} reshape(bf16[256,10,1280]{2,1,0:T(8,128)(2,1)} %copy.56) | data formatting | bytes 13107200 | tf_op jit(solution)/shard_map/reshape | solution.py:88
  255.6 8.9 %multiply_reduce_fusion = (bf16[2560]{0:T(1024)(128)(2,1)S(1)}, bf16[2560,320]{0,1:T(8,128)(2,1)S(1)}) fusion(f32[2560,320]{0,1:T(8,128)} %fusion.15, f32[2560]{0:T(1024)S(1)} %add_divide_fusion, bf16[2560,1280]{1,0:T(8,128)(2,1)} %reshape.188, bf16[1,320,1280]{2,1,0:T(8,128)(2,1)S(1)} %copy-done.14), kind=kOutput, calls=%fused_computation.16 | convolution fusion | flops 2117629440 | bytes 12303360 | tf_op jit(solution)/shard_map/dot_general | solution.py:46
  264.6 5.6 convolution_convert_fusion
  270.2 0.6 copy-done.16
  270.8 0.6 dynamic-slice
  271.4 7.0 %all-reduce = bf16[4,640]{1,0:T(4,128)(2,1)S(1)} all-reduce(bf16[4,640]{1,0:T(4,128)(2,1)S(1)} %convert_element_type.107), channel_id=5, replica_groups=mesh['expert'=64,'dp'=4] {'dp'}, use_global_device_ids=true, to_apply=%region_9.10.clone | all-reduce | flops 2560 | bytes 10240
  278.4 0.7 dynamic-slice_reduce_fusion
  279.1 0.8 convert_element_type.119
  279.9 13.2 %all-to-all-start.3 = ((bf16[64,1,10]{2,1,0:T(2,128)(2,1)}), bf16[64,1,10]{2,1,0:T(2,128)(2,1)S(1)}, u32[]{:S(2)}, u32[]{:S(2)}) async-start(bf16[64,1,10]{2,1,0:T(2,128)(2,1)} %convert_element_type.119), calls=%async_computation.4 | async-start | bytes 65536 | tf_op jit(solution)/shard_map/all_to_all | solution.py:112
  293.1 46.7 %reduce-scatter.2.cloned.1.call-done = bf16[1,640,1280]{2,1,0:T(8,128)(2,1)} async-done(((bf16[4,640,1280]{2,1,0:T(8,128)(2,1)}), bf16[1,640,1280]{2,1,0:T(8,128)(2,1)}) %reduce-scatter.2.cloned.1.call-update) | async-done | bytes 1638416 | tf_op jit(solution)/shard_map/reduce_scatter | solution.py:91
  339.8 4.0 convert_element_type.103
  343.8 0.6 copy-done.7
  344.4 10.7 %all-to-all-start.2 = ((bf16[64,10,1280]{2,1,0:T(8,128)(2,1)}), bf16[64,10,1280]{2,1,0:T(8,128)(2,1)S(1)}, u32[]{:S(2)}, u32[]{:S(2)}) async-start(bf16[64,10,1280]{2,1,0:T(8,128)(2,1)} %convert_element_type.103), calls=%async_computation.3 | async-start | bytes 5242880 | tf_op jit(solution)/shard_map/all_to_all | solution.py:109
  355.2 0.8 reduce_sum.115
  356.0 0.7 copy.58
  356.7 1.0 mul.193
  357.7 1.4 copy.51
  359.1 1.1 fusion.41
  360.3 0.7 select_reduce_fusion.2
  360.9 6.7 %fusion.10 = bf16[1,1280,320]{1,2,0:T(8,128)(2,1)} fusion(bf16[2560,320]{0,1:T(8,128)(2,1)} %copy-done.15, bf16[2560,1280]{1,0:T(8,128)(2,1)} %reshape.183), kind=kOutput, calls=%fused_computation.22 | convolution fusion | flops 2097561600 | bytes 9011200 | tf_op jit(solution)/shard_map/dot_general | solution.py:51
  367.6 6.9 %fusion.11 = bf16[1,320,1280]{2,1,0:T(8,128)(2,1)} fusion(bf16[2560,1280]{1,0:T(8,128)(2,1)} %reshape.188, f32[2560]{0:T(1024)S(1)} %add_divide_fusion, f32[2560,320]{0,1:T(8,128)S(1)} %copy-done.17), kind=kOutput, calls=%fused_computation.23 | convolution fusion | flops 2114764800 | bytes 10659840 | tf_op jit(solution)/shard_map/dot_general | solution.py:50
  374.5 0.6 convert_element_type.118
  375.2 0.8 reduce_sum.120
  376.1 2.2 gather_fusion.1
  378.3 0.8 gather.15
  379.1 0.9 copy.60
  380.0 1.3 subtract_multiply_fusion
  381.3 0.7 copy.52
  382.0 0.7 select_reduce_fusion.1
  382.7 1.9 fusion.42
  384.6 31.6 %all-to-all-done.2 = bf16[64,10,1280]{2,1,0:T(8,128)(2,1)S(1)} async-done(((bf16[64,10,1280]{2,1,0:T(8,128)(2,1)}), bf16[64,10,1280]{2,1,0:T(8,128)(2,1)S(1)}, u32[]{:S(2)}, u32[]{:S(2)}) %all-to-all-start.2) | async-done | bytes 1638432 | tf_op jit(solution)/shard_map/all_to_all | solution.py:109
  416.2 2.0 convert_reduce_fusion
  418.2 1.9 reshape.191
  420.1 2.2 gather_fusion
  422.3 2.1 gather.13
  424.5 1.7 select_reduce_fusion
  426.2 0.7 fusion.31
  427.0 1.0 fusion.30
  428.0 75.6 %psum.15 = f32[1280]{0:T(1024)} all-reduce(f32[1280]{0:T(1024)S(1)} %get-tuple-element.5), channel_id=1, replica_groups=mesh['expert'=64,'dp'=4] {'expert','dp'}, use_global_device_ids=true, to_apply=%region_17.18 | all-reduce | flops 1280 | bytes 10240 | tf_op jit(solution)/shard_map/psum | solution.py:131
  503.6 130.3 %all-reduce.3.cloned.1.call-done = f32[1280,32]{0,1:T(8,128)} async-done(((f32[1280,32]{0,1:T(8,128)}), f32[1280,32]{0,1:T(8,128)}) %all-reduce.3.cloned.1.call-update) | async-done | bytes 163856 | tf_op jit(solution)/shard_map/psum | solution.py:131
  634.0 1.6 copy.69
  (63 shorter events, 1.8 us)
Async XLA Ops:
  7.2 186.0 %copy-start = (bf16[1,1280,320]{1,2,0:T(8,128)(2,1)S(1)}, bf16[1,1280,320]{1,2,0:T(8,128)(2,1)}, u32[]{:S(2)}) copy-start(bf16[1,1280,320]{1,2,0:T(8,128)(2,1)} %param.11) | copy-start | bytes 2457604
  7.2 156.7 %all-gather.5.cloned.1.call-start = ((), (), s32[]{:S(2)}) async-start(), calls=%async_computation.7 | async-start | bytes 8192000 | tf_op jit(solution)/shard_map/all_gather | solution.py:84
  11.6 3.3 copy-start.12
  12.9 0.7 copy-start.3
  90.8 1.7 copy-start.4
  92.5 139.5 %all-gather.7.cloned.1.call-start = ((), (), s32[]{:S(2)}) async-start(), calls=%async_computation.8 | async-start | bytes 8192000 | tf_op jit(solution)/shard_map/all_gather | solution.py:85
  163.8 176.0 %reduce-scatter.2.cloned.1.call-start = ((), (), s32[]{:S(2)}) async-start(), calls=%async_computation.5 | async-start | bytes 8192000 | tf_op jit(solution)/shard_map/reduce_scatter | solution.py:91
  175.2 13.0 %copy-start.6 = (bf16[1280,32]{0,1:T(8,128)(2,1)S(1)}, bf16[1280,32]{0,1:T(8,128)(2,1)}, u32[]{:S(2)}) copy-start(bf16[1280,32]{0,1:T(8,128)(2,1)} %param.9) | copy-start | bytes 245764
  188.2 5.0 copy-start.1
  242.8 12.8 %copy-start.14 = (bf16[1,320,1280]{2,1,0:T(8,128)(2,1)S(1)}, bf16[1,320,1280]{2,1,0:T(8,128)(2,1)}, u32[]{:S(2)}) copy-start(bf16[1,320,1280]{2,1,0:T(8,128)(2,1)} %param.12) | copy-start | bytes 2457604
  264.6 5.6 copy-start.15
  270.1 0.7 copy-start.16
  279.9 63.9 %all-to-all-start.3 = ((bf16[64,1,10]{2,1,0:T(2,128)(2,1)}), bf16[64,1,10]{2,1,0:T(2,128)(2,1)S(1)}, u32[]{:S(2)}, u32[]{:S(2)}) async-start(bf16[64,1,10]{2,1,0:T(2,128)(2,1)} %convert_element_type.119), calls=%async_computation.4 | async-start | bytes 65536 | tf_op jit(solution)/shard_map/all_to_all | solution.py:112
  343.8 12.2 %copy-start.11 = (s32[128,2]{0,1:T(2,128)S(1)}, s32[128,2]{0,1:T(2,128)}, u32[]{:S(2)}) copy-start(s32[128,2]{0,1:T(2,128)} %param.10) | copy-start | bytes 3076
  343.8 0.6 copy-start.7
  344.4 71.8 %all-to-all-start.2 = ((bf16[64,10,1280]{2,1,0:T(8,128)(2,1)}), bf16[64,10,1280]{2,1,0:T(8,128)(2,1)S(1)}, u32[]{:S(2)}, u32[]{:S(2)}) async-start(bf16[64,10,1280]{2,1,0:T(8,128)(2,1)} %convert_element_type.103), calls=%async_computation.3 | async-start | bytes 5242880 | tf_op jit(solution)/shard_map/all_to_all | solution.py:109
  355.1 278.8 %all-reduce.3.cloned.1.call-start = ((), (), s32[]{:S(2)}) async-start(), calls=%async_computation.6 | async-start | bytes 327680 | tf_op jit(solution)/shard_map/psum | solution.py:131
  360.9 6.7 %copy-start.17 = (f32[2560,320]{0,1:T(8,128)S(1)}, f32[2560,320]{0,1:T(8,128)}, u32[]{:S(2)}) copy-start(f32[2560,320]{0,1:T(8,128)} %fusion.15) | copy-start | bytes 9830404
  367.6 6.9 %copy-start.8 = (bf16[64,1,10]{2,1,0:T(2,128)(2,1)S(1)}, bf16[64,1,10]{2,1,0:T(2,128)(2,1)}, u32[]{:S(2)}) copy-start(bf16[64,1,10]{2,1,0:T(2,128)(2,1)} %copy-done.7) | copy-start | bytes 3844
  420.1 4.4 copy-start.10
  422.3 3.9 copy-start.2
  422.3 3.9 copy-start.9
  422.3 3.9 copy-start.13
  422.3 4.6 copy-start.5
Sparse Core Ops, SparseCore 0:
  92.6 66.4 all-gather.4
  164.0 67.9 all-gather.6
  270.3 69.4 reduce-scatter.1
  384.7 249.2 all-reduce.2
where the time goes:
time: 644 us; the launch traced here: 642 us
  waiting for transfers between devices  243 us (38%)
  blocking collectives  226 us (35%)
  local copies, waits for them, and re-layouts  79.3 us (12%)
  matrix products  41.6 us (6%)
  starting transfers between devices  24.1 us (4%)
  between operations  14.1 us (2%)
  other arithmetic  13.1 us (2%)
    psum x1, waiting for transfers between devices, body(): lax.psum((router_term, gain_product), ('expert', 'dp'))  130 us
    all_to_all x1, blocking collectives, body(): lax.all_to_all(send_m, 'expert', split_axis=0, concat_axis=0, tiled=True)  75.7 us
    psum x1, blocking collectives, body(): lax.psum((router_term, gain_product), ('expert', 'dp'))  75.6 us
    all_to_all x1, blocking collectives, body(): lax.all_to_all(send_d, 'expert', split_axis=0, concat_axis=0, tiled=True)  68.1 us
    reduce_scatter x1, waiting for transfers between devices, body(): lax.psum_scatter(row_gradient.reshape(groups, halves * expert_capacity, w...  46.7 us
    all_gather x1, waiting for transfers between devices, body(): lax.all_gather(recv_d[None], 'dp', axis=0, tiled=True)  34.7 us
    all_to_all x1, waiting for transfers between devices, body(): lax.all_to_all(back_rows.astype(jnp.bfloat16), 'expert', split_axis=0, co...  31.6 us
    all_to_all x1, starting transfers between devices, body(): lax.all_to_all(back_gate.astype(jnp.bfloat16), 'expert', split_axis=0, co...  13.2 us
  transfers between devices with their start and end apart: 6, of which 4 were waited for; matrix products, arithmetic and copies ran while one was open for 13% of the time, Pallas kernels for 0%

commit v1 on v0

--- a/solution.py
+++ b/solution.py
@@ -82,7 +82,12 @@
     column = lax.dynamic_slice_in_dim(router, own, 1, 1)
     all_m, all_d = (
         lax.all_gather(recv_m[None], "dp", axis=0, tiled=True),
-        lax.all_gather(recv_d[None], "dp", axis=0, tiled=True),
+        jnp.concatenate(
+            jax.lax.all_to_all(
+                jnp.stack([recv_d[None]] * jax.lax.axis_size("dp"), axis=0), "dp", 0, 0
+            ),
+            axis=0,
+        ),
     )
     row_gradient, gate_gradient, grad_first, grad_second = expert_pass(
         all_m.reshape(-1, width), all_d.reshape(-1, width), column, w_in[0], w_out[0]

time: 644 us -> 687 us (1.067); the launches traced: 642 us -> 677 us
  waiting for transfers between devices: 243 us -> 282 us
  matrix products: 41.6 us -> 34.7 us
    all_to_all x0 -> x1, waiting for transfers between devices: none -> 73.9 us  [body(): jax.lax.all_to_all(jnp.stack([recv_d[None]] * jax.lax.axis_size('dp'), ax...]
    all_gather x1 -> x0, waiting for transfers between devices: 34.7 us -> none  [body(): lax.all_gather(recv_d[None], 'dp', axis=0, tiled=True)]
    another operation x1 -> x3, local copies, waits for them, and re-layouts: 0.01 us -> 16.5 us  [the longest x1 12.9 us: body(): all_d.reshape(-1, width)]
    reshape x1 -> x0, local copies, waits for them, and re-layouts: 12.8 us -> none  [body(): all_d.reshape(-1, width)]
    all_to_all x0 -> x1, local copies, waits for them, and re-layouts: none -> 10.9 us  [body(): jax.lax.all_to_all(jnp.stack([recv_d[None]] * jax.lax.axis_size('dp'), ax...]
    all_gather x1 -> x0, local copies, waits for them, and re-layouts: 10.8 us -> none  [body(): lax.all_gather(recv_d[None], 'dp', axis=0, tiled=True)]
  transfers between devices with their start and end apart: 6 -> 6, of which waited for: 4 -> 4; matrix products, arithmetic and copies ran while one was open for 13% -> 11% of each run, Pallas kernels for 0% -> 0%
where the time goes in v1:
time: 687 us; the launch traced here: 677 us
  waiting for transfers between devices  282 us (41%)
  blocking collectives  226 us (33%)
  local copies, waits for them, and re-layouts  82.2 us (12%)
  matrix products  34.7 us (5%)
  starting transfers between devices  24.3 us (4%)
  between operations  14.6 us (2%)
  other arithmetic  13.2 us (2%)
    psum x1, waiting for transfers between devices, body(): lax.psum((router_term, gain_product), ('expert', 'dp'))  130 us
    all_to_all x1, blocking collectives, body(): lax.all_to_all(send_m, 'expert', split_axis=0, concat_axis=0, tiled=True)  75.7 us
    psum x1, blocking collectives, body(): lax.psum((router_term, gain_product), ('expert', 'dp'))  75.6 us
    all_to_all x1, waiting for transfers between devices, body(): jax.lax.all_to_all(jnp.stack([recv_d[None]] * jax.lax.axis_size('dp'), ax...  73.9 us
    all_to_all x1, blocking collectives, body(): lax.all_to_all(send_d, 'expert', split_axis=0, concat_axis=0, tiled=True)  68.1 us
    reduce_scatter x1, waiting for transfers between devices, body(): lax.psum_scatter(row_gradient.reshape(groups, halves * expert_capacity, w...  45.8 us
    all_to_all x1, waiting for transfers between devices, body(): lax.all_to_all(back_rows.astype(jnp.bfloat16), 'expert', split_axis=0, co...  31.7 us
  transfers between devices with their start and end apart: 6, of which 4 were waited for; matrix products, arithmetic and copies ran while one was open for 11% of the time, Pallas kernels for 0%

profile of v1, /device:TPU:1, one launch (start us, length us, event | category | flops | bytes accessed | tf_op | source)
XLA Modules:
  0.0 677.2 jit_solution(9703003714067009764)
XLA Ops:
  7.2 0.9 copy.48
  8.4 0.6 reduce-window.6
  9.3 1.1 convert_reduce_fusion.1
  10.4 1.2 fusion.32
  11.6 1.2 fusion.25
  12.9 0.7 copy-done.3
  13.6 0.3 broadcast_in_dim.27
  14.2 0.4 convolution_convert_fusion.3
  15.1 75.7 %all_to_all.26 = bf16[64,10,1280]{2,1,0:T(8,128)(2,1)S(1)} all-to-all(bf16[64,10,1280]{2,1,0:T(8,128)(2,1)S(1)} %bitcast.62), channel_id=1, replica_groups=mesh['expert'=64,'dp'=4] {'expert'}, dimensions={0} | all-to-all | bytes 3276800 | tf_op jit(solution)/shard_map/all_to_all | solution.py:78
  90.8 1.7 copy.53
  92.5 0.3 broadcast_in_dim.30
  93.1 0.4 convolution_convert_fusion.2
  94.0 68.1 %all_to_all.27 = bf16[64,10,1280]{2,1,0:T(8,128)(2,1)S(1)} all-to-all(bf16[64,10,1280]{2,1,0:T(8,128)(2,1)S(1)} %bitcast.63), channel_id=1, replica_groups=mesh['expert'=64,'dp'=4] {'expert'}, dimensions={0} | all-to-all | bytes 3276800 | tf_op jit(solution)/shard_map/all_to_all | solution.py:79
  162.1 0.5 copy.55
  162.6 3.5 stack.3
  166.1 5.3 all-to-all-start.2
  171.5 73.9 %all-to-all-done.2 = bf16[4,1,64,10,1280]{4,2,3,1,0:T(8,128)(2,1)} async-done(((bf16[4,1,64,10,1280]{4,2,3,1,0:T(8,128)(2,1)}), bf16[4,1,64,10,1280]{4,2,3,1,0:T(8,128)(2,1)}, u32[]{:S(2)}, u32[]{:S(2)}) %all-to-all-start.2) | async-done | bytes 6553632 | tf_op jit(solution)/shard_map/all_to_all | solution.py:86
  245.3 10.9 %copy.56 = bf16[4,1,64,10,1280]{4,3,2,0,1:T(8,128)(2,1)} copy(bf16[4,1,64,10,1280]{4,2,3,1,0:T(8,128)(2,1)} %all-to-all-done.2) | data formatting | bytes 13107200 | tf_op jit(solution)/shard_map/all_to_all | solution.py:86
  256.2 12.9 %reshape_reshape.3 = bf16[2560,1280]{1,0:T(8,128)(2,1)} reshape(bf16[4,1,64,10,1280]{4,3,2,0,1:T(8,128)(2,1)} %copy.56) | data formatting | bytes 13107200 | tf_op jit(solution)/shard_map/reshape;reshape | solution.py:93
  269.2 10.8 %copy.54 = bf16[256,10,1280]{2,1,0:T(8,128)(2,1)} copy(bf16[256,10,1280]{2,0,1:T(8,128)(2,1)} %all-gather.3.cloned.1.call-done) | data formatting | bytes 13107200 | tf_op jit(solution)/shard_map/all_gather | solution.py:84
  280.0 12.8 %reshape.182 = bf16[2560,1280]{1,0:T(8,128)(2,1)} reshape(bf16[256,10,1280]{2,1,0:T(8,128)(2,1)} %copy.54) | data formatting | bytes 13107200 | tf_op jit(solution)/shard_map/reshape | solution.py:93
  292.8 4.8 convolution_reduce_fusion
  297.7 2.3 fusion.15
  300.1 4.0 multiply_reduce_fusion
  304.1 1.2 copy-done.15
  305.3 5.5 convolution_convert_fusion
  310.8 0.6 copy-done.16
  311.5 0.6 dynamic-slice
  312.1 7.0 %all-reduce = bf16[4,640]{1,0:T(4,128)(2,1)S(1)} all-reduce(bf16[4,640]{1,0:T(4,128)(2,1)S(1)} %convert_element_type.107), channel_id=4, replica_groups=mesh['expert'=64,'dp'=4] {'dp'}, use_global_device_ids=true, to_apply=%region_9.10.clone | all-reduce | flops 2560 | bytes 10240
  319.1 0.7 dynamic-slice_reduce_fusion
  319.7 0.8 convert_element_type.119
  320.5 8.1 %all-to-all-start.4 = ((bf16[64,1,10]{2,1,0:T(2,128)(2,1)}), bf16[64,1,10]{2,1,0:T(2,128)(2,1)S(1)}, u32[]{:S(2)}, u32[]{:S(2)}) async-start(bf16[64,1,10]{2,1,0:T(2,128)(2,1)} %convert_element_type.119), calls=%async_computation.5 | async-start | bytes 65536 | tf_op jit(solution)/shard_map/all_to_all | solution.py:117
  328.6 45.8 %reduce-scatter.2.cloned.1.call-done = bf16[1,640,1280]{2,1,0:T(8,128)(2,1)} async-done(((bf16[4,640,1280]{2,1,0:T(8,128)(2,1)}), bf16[1,640,1280]{2,1,0:T(8,128)(2,1)}) %reduce-scatter.2.cloned.1.call-update) | async-done | bytes 1638416 | tf_op jit(solution)/shard_map/reduce_scatter | solution.py:96
  374.4 4.0 convert_element_type.103
  378.4 0.6 copy-done.7
  379.0 10.9 %all-to-all-start.3 = ((bf16[64,10,1280]{2,1,0:T(8,128)(2,1)}), bf16[64,10,1280]{2,1,0:T(8,128)(2,1)S(1)}, u32[]{:S(2)}, u32[]{:S(2)}) async-start(bf16[64,10,1280]{2,1,0:T(8,128)(2,1)} %convert_element_type.103), calls=%async_computation.4 | async-start | bytes 5242880 | tf_op jit(solution)/shard_map/all_to_all | solution.py:114
  389.9 0.8 reduce_sum.115
  390.7 0.7 copy.58
  391.5 1.0 mul.193
  392.4 1.5 copy.51
  394.0 1.1 fusion.41
  395.1 0.7 select_reduce_fusion.2
  395.8 6.7 fusion.10
  402.4 6.9 %fusion.11 = bf16[1,320,1280]{2,1,0:T(8,128)(2,1)} fusion(bf16[2560,1280]{1,0:T(8,128)(2,1)} %reshape_reshape.3, f32[2560]{0:T(1024)S(1)} %add_divide_fusion, f32[2560,320]{0,1:T(8,128)S(1)} %copy-done.18), kind=kOutput, calls=%fused_computation.23 | convolution fusion | flops 2114764800 | bytes 10659840 | tf_op jit(solution)/shard_map/dot_general | solution.py:50
  409.4 0.6 convert_element_type.118
  410.0 0.8 reduce_sum.120
  410.9 1.9 gather_fusion.1
  412.9 0.8 gather.15
  413.6 0.9 copy.60
  414.5 1.3 subtract_multiply_fusion
  415.8 0.7 copy.52
  416.6 0.7 select_reduce_fusion.1
  417.3 1.9 fusion.42
  419.2 31.7 %all-to-all-done.3 = bf16[64,10,1280]{2,1,0:T(8,128)(2,1)S(1)} async-done(((bf16[64,10,1280]{2,1,0:T(8,128)(2,1)}), bf16[64,10,1280]{2,1,0:T(8,128)(2,1)S(1)}, u32[]{:S(2)}, u32[]{:S(2)}) %all-to-all-start.3) | async-done | bytes 1638432 | tf_op jit(solution)/shard_map/all_to_all | solution.py:114
  450.9 2.0 convert_reduce_fusion
  452.9 1.9 reshape.189
  454.8 2.2 gather_fusion
  457.1 2.1 gather.13
  459.2 1.7 select_reduce_fusion
  461.0 0.7 fusion.31
  461.7 1.0 fusion.30
  462.8 75.6 %psum.15 = f32[1280]{0:T(1024)} all-reduce(f32[1280]{0:T(1024)S(1)} %get-tuple-element.5), channel_id=1, replica_groups=mesh['expert'=64,'dp'=4] {'expert','dp'}, use_global_device_ids=true, to_apply=%region_17.18 | all-reduce | flops 1280 | bytes 10240 | tf_op jit(solution)/shard_map/psum | solution.py:136
  538.3 130.4 %all-reduce.3.cloned.1.call-done = f32[1280,32]{0,1:T(8,128)} async-done(((f32[1280,32]{0,1:T(8,128)}), f32[1280,32]{0,1:T(8,128)}) %all-reduce.3.cloned.1.call-update) | async-done | bytes 163856 | tf_op jit(solution)/shard_map/psum | solution.py:136
  668.7 1.6 copy.69
  (70 shorter events, 2.6 us)
Async XLA Ops:
  7.2 290.5 %copy-start = (bf16[1,1280,320]{1,2,0:T(8,128)(2,1)S(1)}, bf16[1,1280,320]{1,2,0:T(8,128)(2,1)}, u32[]{:S(2)}) copy-start(bf16[1,1280,320]{1,2,0:T(8,128)(2,1)} %param.11) | copy-start | bytes 2457604
  7.2 262.0 %all-gather.3.cloned.1.call-start = ((), (), s32[]{:S(2)}) async-start(), calls=%async_computation.8 | async-start | bytes 8192000 | tf_op jit(solution)/shard_map/all_gather | solution.py:84
  11.6 3.3 copy-start.12
  12.9 0.7 copy-start.3
  90.8 1.7 copy-start.4
  166.1 79.2 %all-to-all-start.2 = ((bf16[4,1,64,10,1280]{4,2,3,1,0:T(8,128)(2,1)}), bf16[4,1,64,10,1280]{4,2,3,1,0:T(8,128)(2,1)}, u32[]{:S(2)}, u32[]{:S(2)}) async-start(bf16[4,1,64,10,1280]{4,2,3,1,0:T(8,128)(2,1)} %stack.3), calls=%async_computation.2 | async-start | bytes 13107200 | tf_op jit(solution)/shard_map/all_to_all | solution.py:86
  171.4 203.0 %reduce-scatter.2.cloned.1.call-start = ((), (), s32[]{:S(2)}) async-start(), calls=%async_computation.6 | async-start | bytes 8192000 | tf_op jit(solution)/shard_map/reduce_scatter | solution.py:96
  280.0 12.8 %copy-start.6 = (bf16[1280,32]{0,1:T(8,128)(2,1)S(1)}, bf16[1280,32]{0,1:T(8,128)(2,1)}, u32[]{:S(2)}) copy-start(bf16[1280,32]{0,1:T(8,128)(2,1)} %param.9) | copy-start | bytes 245764
  292.8 4.9 copy-start.1
  292.8 7.2 %slice-start = ((s8[6553600]{0:T(1024)(128)(4,1)}), s8[4194304]{0:T(1024)(128)(4,1)S(1)}, s32[]{:S(2)}) async-start(s8[6553600]{0:T(1024)(128)(4,1)} %bitcast.64), calls=%async_computation.9 | async-start | bytes 8388608
  297.7 2.4 slice-start.1
  297.7 2.4 copy-start.14
  300.1 4.0 copy-start.17
  304.1 1.2 copy-start.15
  310.8 0.7 copy-start.16
  320.5 57.9 %all-to-all-start.4 = ((bf16[64,1,10]{2,1,0:T(2,128)(2,1)}), bf16[64,1,10]{2,1,0:T(2,128)(2,1)S(1)}, u32[]{:S(2)}, u32[]{:S(2)}) async-start(bf16[64,1,10]{2,1,0:T(2,128)(2,1)} %convert_element_type.119), calls=%async_computation.5 | async-start | bytes 65536 | tf_op jit(solution)/shard_map/all_to_all | solution.py:117
  378.4 12.3 %copy-start.11 = (s32[128,2]{0,1:T(2,128)S(1)}, s32[128,2]{0,1:T(2,128)}, u32[]{:S(2)}) copy-start(s32[128,2]{0,1:T(2,128)} %param.10) | copy-start | bytes 3076
  378.4 0.6 copy-start.7
  379.0 71.9 %all-to-all-start.3 = ((bf16[64,10,1280]{2,1,0:T(8,128)(2,1)}), bf16[64,10,1280]{2,1,0:T(8,128)(2,1)S(1)}, u32[]{:S(2)}, u32[]{:S(2)}) async-start(bf16[64,10,1280]{2,1,0:T(8,128)(2,1)} %convert_element_type.103), calls=%async_computation.4 | async-start | bytes 5242880 | tf_op jit(solution)/shard_map/all_to_all | solution.py:114
  389.9 278.8 %all-reduce.3.cloned.1.call-start = ((), (), s32[]{:S(2)}) async-start(), calls=%async_computation.7 | async-start | bytes 327680 | tf_op jit(solution)/shard_map/psum | solution.py:136
  395.8 6.7 copy-start.18
  402.4 6.9 %copy-start.8 = (bf16[64,1,10]{2,1,0:T(2,128)(2,1)S(1)}, bf16[64,1,10]{2,1,0:T(2,128)(2,1)}, u32[]{:S(2)}) copy-start(bf16[64,1,10]{2,1,0:T(2,128)(2,1)} %copy-done.7) | copy-start | bytes 3844
  454.8 4.4 copy-start.10
  457.1 3.9 copy-start.2
  457.1 3.9 copy-start.9
  457.1 3.9 copy-start.13
  457.1 4.6 copy-start.5
Sparse Core Ops, SparseCore 0:
  92.6 66.4 all-gather.2
  310.9 63.4 reduce-scatter.1
  419.3 249.3 all-reduce.2
